TPU v7x, 256 devices: a whole 4x4x8 slice. The times are simulated.
256 devices in a mesh: seq: 32 (over z, x), head: 8 (over y, core).
Axes of the slice: x: 4, y: 4, z: 8, core: 2. Of those that a mesh axis runs over, the one named last changes fastest.
Arguments:
- corpus: bfloat16 [128, 128, 4096], P('seq'), may hold values from -8 to 8
- enc_qkv: bfloat16 [4096, 16, 3, 128], P(None, 'head'), may hold values from -0.1015625 to 0.1015625
- enc_out: bfloat16 [16, 128, 4096], P('head'), may hold values from -0.375 to 0.375
- cca_kv: bfloat16 [4096, 16, 2, 128], P('seq', 'head'), may hold values from -0.09375 to 0.09375
- gain_in: float32 [4096], replicated, may hold values from 0.5 to 2
- gain_out: float32 [4096], replicated, may hold values from 0.5 to 2
- queries: bfloat16 [16384, 16, 128], P('seq', 'head'), may hold values from -100 to 100
- nbr_ids: int32 [256, 2], P('seq'), may hold values from 0 to 127, as said below
Outputs:
- cca_out: bfloat16 [16384, 16, 128], P('seq', 'head')
Inputs may be any that keep to these rules, and one draw needn't show every extreme that they name: `nbr_ids`: entry [u, n] is the corpus row of group u's n-th neighbour; row r is held by index r // 4 of seq. The neighbours of one group differ. Among the requests of the 8 groups of one index of seq no owner is named more than 2 times, and in every draw some owner is named exactly 2 times by every index of seq.
All inputs are finite; a program needn't handle non-finite values.
Results may differ from a plain program's by a relative error of at most 0.03.
Values may be sent and summed in bfloat16 or wider, within the bound.
No kernel may reach another device: no remote copies, remote signals or barrier semaphores. Data moves between devices by JAX's collectives and lax.ppermute only.
A program may use at most 128 MiB of HBM per device.

v0:
```python
import jax
import jax.numpy as jnp
from jax import lax
from jax.sharding import PartitionSpec as P

GROUP = 64
NBRS = 2
CAP = 2
EPS = 1e-06


def passed_along(value, axis, steps):
    count = lax.axis_size(axis)
    first, last = (max(0, -steps), min(count, count - steps))
    return lax.ppermute(value, axis, [(source, source + steps) for source in range(first, last)])


def rms_scale(values, gain):
    mean_square = jnp.mean(values * values, axis=-1, keepdims=True)
    return values * lax.rsqrt(mean_square + EPS) * gain


def attend(query_blocks, key_blocks, value_blocks):
    scale = query_blocks.shape[-1] ** (-0.5)
    scores = (
        jnp.einsum("bqhs,bkhs->bhqk", query_blocks, key_blocks, preferred_element_type=jnp.float32)
        * scale
    )
    probs = jax.nn.softmax(scores, axis=-1).astype(jnp.bfloat16)
    return jnp.einsum("bhqk,bkhs->bqhs", probs, value_blocks, preferred_element_type=jnp.float32)


def on_device(corpus, enc_qkv, enc_out, cca_kv, gain_in, gain_out, queries, nbr_ids):
    corp_rows, row_tokens, model_width = corpus.shape
    heads_here = enc_qkv.shape[1]
    head_size = enc_qkv.shape[3]
    row_total = corp_rows * row_tokens
    corpus_flat = corpus.reshape(row_total, model_width)
    normed_in = rms_scale(corpus_flat.astype(jnp.float32), gain_in).astype(jnp.bfloat16)
    projected = jnp.dot(
        normed_in,
        enc_qkv.reshape(model_width, heads_here * 3 * head_size),
        preferred_element_type=jnp.float32,
    )
    projected = projected.astype(jnp.bfloat16).reshape(
        corp_rows, row_tokens, heads_here, 3, head_size
    )
    attended = attend(projected[:, :, :, 0], projected[:, :, :, 1], projected[:, :, :, 2]).astype(
        jnp.bfloat16
    )
    attended = attended.reshape(row_total, heads_here * head_size)
    out_weight = enc_out.reshape(heads_here * head_size, model_width)
    partial_terms = jnp.dot(attended, out_weight, preferred_element_type=jnp.float32)
    enc_sum = lax.psum(partial_terms, "head")
    normed = rms_scale(corpus_flat.astype(jnp.float32) + enc_sum, gain_out).astype(jnp.bfloat16)
    memory_cols = heads_here * 2 * head_size
    shard_piece = lax.all_gather(cca_kv, "seq", axis=0, tiled=True)
    memory = jnp.dot(
        normed,
        shard_piece.reshape(shard_piece.shape[0], memory_cols),
        preferred_element_type=jnp.float32,
    )
    memory = memory.astype(jnp.bfloat16).reshape(corp_rows, row_tokens, heads_here, 2, head_size)
    request_ids = nbr_ids.reshape(-1)
    demand = request_ids.shape[0]
    owners = request_ids // corp_rows
    local_row = request_ids % corp_rows
    request_order = jnp.arange(demand)
    earlier = request_order[None, :] < request_order[:, None]
    same_owner = owners[:, None] == owners[None, :]
    slot_rank = jnp.sum(jnp.logical_and(same_owner, earlier), axis=1)
    slot_index = owners * CAP + slot_rank
    devices = lax.axis_size("seq")
    positions = jnp.arange(devices * CAP)
    matched = positions[:, None] == slot_index[None, :]
    wanted = jnp.sum(jnp.where(matched, local_row[None, :], 0), axis=1).reshape(devices, CAP)
    picked = jnp.take(
        memory, lax.all_to_all(wanted, "seq", split_axis=0, concat_axis=0, tiled=True), axis=0
    )
    fetched = lax.all_to_all(picked, "seq", split_axis=0, concat_axis=0, tiled=True)
    fetched = fetched.reshape(devices * CAP, row_tokens, heads_here, 2, head_size)
    group_memory = jnp.take(fetched, slot_index, axis=0)
    groups_here = nbr_ids.shape[0]
    group_memory = group_memory.reshape(groups_here, NBRS * row_tokens, heads_here, 2, head_size)
    token_count = queries.shape[0]
    lead = GROUP - 1
    before = passed_along(group_memory[groups_here - 1 :], "seq", 1)
    window_memory = jnp.concatenate([before, group_memory], axis=0)
    padded_queries = jnp.concatenate(
        [
            jnp.zeros((1, heads_here, head_size), jnp.bfloat16),
            queries,
            jnp.zeros((lead, heads_here, head_size), jnp.bfloat16),
        ],
        axis=0,
    ).reshape(groups_here + 1, GROUP, heads_here, head_size)
    extended = attend(padded_queries, window_memory[:, :, :, 0], window_memory[:, :, :, 1])
    extended = extended.reshape((groups_here + 1) * GROUP, heads_here, head_size)
    result = extended[1 : 1 + token_count].astype(jnp.bfloat16)
    return result


def solution(mesh):
    placed = (
        P("seq", None, None),
        P(None, "head", None, None),
        P("head", None, None),
        P("seq", "head", None, None),
        P(),
        P(),
        P("seq", "head", None),
        P("seq", None),
    )
    return jax.shard_map(
        on_device, mesh=mesh, in_specs=placed, out_specs=P("seq", "head", None), check_vma=False
    )
```

profile of v0, /device:TPU:104, one launch (start us, length us, event | category | flops | bytes accessed | tf_op | source)
XLA Modules:
  0.0 442.4 jit_solution(8818635364731222058)
XLA Ops:
  7.4 16.4 %copy.108 = bf16[4096,2,3,128]{0,3,2,1:T(8,128)(2,1)} copy(bf16[4096,2,3,128]{3,1,2,0:T(2,128)(2,1)} %param.9) | data formatting | bytes 12582912 | tf_op args[1]
  23.8 3.2 multiply_reduce_fusion.1
  27.0 0.2 copy-done.2
  27.2 1.7 multiply_convert_fusion.1
  28.9 1.1 copy-done.3
  30.0 3.5 convolution_convert_fusion
  33.5 1.2 copy.109
  34.6 1.7 reshape.286
  36.4 1.0 fusion.50
  37.4 0.2 copy.129
  37.6 0.2 copy.130
  37.8 0.3 convolution_multiply_fusion.1
  38.1 0.4 fusion.51
  38.5 1.3 fusion.19
  39.7 0.2 copy.114
  39.9 4.5 %fusion.22 = f32[512,4096]{1,0:T(8,128)} fusion(bf16[256,4096]{1,0:T(8,128)(2,1)S(1)} %bitcast.79, bf16[64,8,2,128]{3,2,1,0:T(2,128)(2,1)S(1)} %bitcast.85), kind=kOutput, calls=%fused_computation.38 | convolution fusion | flops 1073741824 | bytes 10747904 | tf_op jit(solution)/shard_map/dot_general | solution.py:53
  44.5 0.5 all-gather.2.cloned.1.call-update
  45.1 0.1 copy.104
  45.2 0.1 reshape.284
  45.3 0.2 convert_reduce_fusion
  45.5 0.1 select_reduce_fusion
  45.5 0.1 all_to_all.13
  45.7 16.9 %all_to_all.20 = s32[32,1,2]{2,1,0:T(1,128)S(1)} all-to-all(s32[32,1,2]{2,1,0:T(1,128)S(1)} %bitcast.88), channel_id=1, replica_groups=mesh['seq'=32,'head'=8] {'seq'}, dimensions={0} | all-to-all | bytes 512 | tf_op jit(solution)/shard_map/all_to_all | solution.py:78
  62.6 0.1 copy.116
  62.7 0.1 reshape.298
  62.9 0.1 copy.107
  63.0 90.3 %all-reduce.2.cloned.1.call-done = f32[512,4096]{1,0:T(8,128)} async-done(((f32[512,4096]{1,0:T(8,128)}), f32[512,4096]{1,0:T(8,128)}) %all-reduce.2.cloned.1.call-update) | async-done | bytes 8388624 | tf_op jit(solution)/shard_map/psum | solution.py:54
  153.3 8.9 %multiply_reduce_fusion = (f32[512]{0:T(512)S(1)}, f32[512,4096]{1,0:T(8,128)}) fusion(f32[512,4096]{1,0:T(8,128)} %all-reduce.2.cloned.1.call-done, bf16[4,128,4096]{2,1,0:T(8,128)(2,1)} %param.8), kind=kLoop, calls=%fused_computation.7 | loop fusion | flops 8388096 | bytes 20973568 | tf_op jit(solution)/shard_map/reduce_sum | solution.py:19
  162.2 7.2 %reshape.289 = bf16[4096,512]{1,0:T(8,128)(2,1)} reshape(bf16[4096,2,2,128]{3,2,1,0:T(2,128)(2,1)} %all-gather.2.cloned.1.call-done) | data formatting | bytes 8388608 | tf_op jit(solution)/shard_map/reshape | solution.py:60
  169.4 6.9 %fusion.7 = bf16[512,512]{1,0:T(8,128)(2,1)S(1)} fusion(bf16[4096,512]{1,0:T(8,128)(2,1)} %reshape.289, f32[512,4096]{1,0:T(8,128)} %get-tuple-element.8, f32[4096]{0:T(1024)S(1)} %copy-done.7, f32[512]{0:T(512)S(1)} %add_rsqrt_fusion), kind=kOutput, calls=%fused_computation.20 | convolution fusion | flops 2154037248 | bytes 13125632 | tf_op jit(solution)/shard_map/dot_general | solution.py:58
  176.3 0.1 reshape.290
  176.5 18.3 %gather_fusion = bf16[64,128,2,2,128]{4,3,2,1,0:T(2,128)(2,1)} fusion(bf16[4,128,2,2,128]{4,3,2,1,0:T(2,128)(2,1)S(1)} %reshape.290, s32[1024]{0:T(1024)S(1)} %pad_clamp_fusion.1), kind=kCustom, calls=%fused_computation | custom fusion | bytes 16777472 | tf_op jit(solution)/shard_map/jit(_take)/gather | solution.py:77
  194.8 7.7 %copy_select_fusion = bf16[32,2,128,2,2,128]{5,2,4,3,1,0:T(8,128)(2,1)} fusion(bf16[32,2,128,2,2,128]{5,4,3,2,1,0:T(2,128)(2,1)} %bitcast.80, pred[32,2]{1,0:T(8,128)(4,1)S(1)} %copy.107), kind=kLoop, calls=%fused_computation.5 | loop fusion | flops 4194304 | bytes 16777280 | tf_op jit(solution)/shard_map/jit(_take)/select_n | solution.py:77
  202.6 10.0 %all-to-all-start.1 = ((bf16[32,2,128,2,2,128]{5,2,4,3,1,0:T(8,128)(2,1)}), bf16[32,2,128,2,2,128]{5,2,4,3,1,0:T(8,128)(2,1)}, u32[]{:S(2)}, u32[]{:S(2)}) async-start(bf16[32,2,128,2,2,128]{5,2,4,3,1,0:T(8,128)(2,1)} %copy_select_fusion), calls=%async_computation.1 | async-start | bytes 16777216 | tf_op jit(solution)/shard_map/all_to_all | solution.py:80
  212.6 0.1 reshape.292
  212.7 0.1 reduce_sum.64
  212.8 0.1 copy.120
  213.2 0.2 maximum_maximum_fusion
  213.4 198.6 %all-to-all-done.1 = bf16[32,2,128,2,2,128]{5,2,4,3,1,0:T(8,128)(2,1)} async-done(((bf16[32,2,128,2,2,128]{5,2,4,3,1,0:T(8,128)(2,1)}), bf16[32,2,128,2,2,128]{5,2,4,3,1,0:T(8,128)(2,1)}, u32[]{:S(2)}, u32[]{:S(2)}) %all-to-all-start.1) | async-done | bytes 8388640 | tf_op jit(solution)/shard_map/all_to_all | solution.py:80
  412.0 4.3 gather_fusion.1
  416.3 0.1 copy.121
  416.4 0.1 slice_select_fusion
  416.6 1.9 collective-permute-start
  418.5 1.6 copy_select_fusion.1
  420.1 8.8 %collective-permute-done = bf16[1,256,2,2,128]{4,1,2,0,3:T(8,128)(2,1)S(1)} collective-permute-done((bf16[1,256,2,2,128]{4,1,2,0,3:T(8,128)(2,1)S(1)}, bf16[1,256,2,2,128]{4,1,2,0,3:T(8,128)(2,1)S(1)}, u32[]{:S(2)}, u32[]{:S(2)}) %collective-permute-start) | collective-permute-done | bytes 262176 | tf_op jit(solution)/shard_map/ppermute | solution.py:15
  428.8 3.1 fusion.56
  431.9 2.0 fusion.16
  434.0 1.0 copy.126
  (38 shorter events, 0.7 us)
Async XLA Ops:
  7.4 32.6 %copy-start = (bf16[2,128,4096]{2,1,0:T(8,128)(2,1)S(1)}, bf16[2,128,4096]{2,1,0:T(8,128)(2,1)}, u32[]{:S(2)}) copy-start(bf16[2,128,4096]{2,1,0:T(8,128)(2,1)} %param.10) | copy-start | bytes 6291460
  7.4 145.9 %all-reduce.2.cloned.1.call-start = ((), (), s32[]{:S(2)}) async-start(), calls=%async_computation.2 | async-start | bytes 16777216 | tf_op jit(solution)/shard_map/psum | solution.py:54
  7.4 19.6 %copy-start.5 = (f32[4096]{0:T(1024)S(1)}, f32[4096]{0:T(1024)}, u32[]{:S(2)}) copy-start(f32[4096]{0:T(1024)} %param.12) | copy-start | bytes 49156
  23.8 3.4 copy-start.2
  27.2 2.8 copy-start.3
  44.4 0.7 copy-start.6
  44.4 117.7 %all-gather.2.cloned.1.call-start = ((), (), s32[]{:S(2)}) async-start(), calls=%async_computation.3 | async-start | bytes 4325376 | tf_op jit(solution)/shard_map/all_gather | solution.py:57
  162.1 7.3 %copy-start.7 = (f32[4096]{0:T(1024)S(1)}, f32[4096]{0:T(1024)}, u32[]{:S(2)}) copy-start(f32[4096]{0:T(1024)} %param.13) | copy-start | bytes 49156
  202.6 10.3 %copy-start.4 = (bf16[512,2,128]{2,1,0:T(2,128)(2,1)S(1)}, bf16[512,2,128]{2,1,0:T(2,128)(2,1)}, u32[]{:S(2)}) copy-start(bf16[512,2,128]{2,1,0:T(2,128)(2,1)} %param.14) | copy-start | bytes 786436
  202.6 209.4 %all-to-all-start.1 = ((bf16[32,2,128,2,2,128]{5,2,4,3,1,0:T(8,128)(2,1)}), bf16[32,2,128,2,2,128]{5,2,4,3,1,0:T(8,128)(2,1)}, u32[]{:S(2)}, u32[]{:S(2)}) async-start(bf16[32,2,128,2,2,128]{5,2,4,3,1,0:T(8,128)(2,1)} %copy_select_fusion), calls=%async_computation.1 | async-start | bytes 16777216 | tf_op jit(solution)/shard_map/all_to_all | solution.py:80
  416.6 12.3 %collective-permute-start = (bf16[1,256,2,2,128]{4,1,2,0,3:T(8,128)(2,1)S(1)}, bf16[1,256,2,2,128]{4,1,2,0,3:T(8,128)(2,1)S(1)}, u32[]{:S(2)}, u32[]{:S(2)}) collective-permute-start(bf16[1,256,2,2,128]{4,1,2,0,3:T(8,128)(2,1)S(1)} %bitcast.87), channel_id=1, source_target_pairs={{0,8},{8,16},{16,24},{24,32},{32,40},{40,48},{48,56},{56,64},{64,7... | collective-permute-start | bytes 786440 | tf_op jit(solution)/shard_map/ppermute | solution.py:15
  428.8 6.1 %copy-start.1 = (bf16[2,128,4096]{2,1,0:T(8,128)(2,1)S(1)}, bf16[2,128,4096]{2,1,0:T(8,128)(2,1)}, u32[]{:S(2)}) copy-start(bf16[2,128,4096]{2,1,0:T(8,128)(2,1)} %param.10) | copy-start | bytes 6291460
Sparse Core Ops, SparseCore 0:
  44.6 108.6 all-reduce.1
Sparse Core Ops, SparseCore 1:
  47.5 83.2 all-gather.1
where the time goes:
time: 443 us; the launch traced here: 442 us
  waiting for transfers between devices  298 us (67%)
  local copies, waits for them, and re-layouts  54.6 us (12%)
  other arithmetic  23.7 us (5%)
  matrix products  21.9 us (5%)
  blocking collectives  16.9 us (4%)
  between operations  15.1 us (3%)
  starting transfers between devices  12 us (3%)
    all_to_all x1, waiting for transfers between devices, on_device(): lax.all_to_all(picked, 'seq', split_axis=0, concat_axis=0, tiled=True)  199 us
    psum x1, waiting for transfers between devices, on_device(): enc_sum = lax.psum(partial_terms, 'head')  90.3 us
    unnamed x21, local copies, waits for them, and re-layouts  18.3 us
    gather x1, local copies, waits for them, and re-layouts, on_device(): jnp.take(memory, lax.all_to_all(wanted, 'seq', split_axis=0, concat_axis=...  18.3 us
    all_to_all x1, blocking collectives, on_device(): lax.all_to_all(wanted, 'seq', split_axis=0, concat_axis=0, tiled=True)  16.9 us
    reduce_sum x2, other arithmetic, rms_scale(): mean_square = jnp.mean(values * values, axis=-1, keepdims=True)  12.1 us
    all_to_all x1, starting transfers between devices, on_device(): lax.all_to_all(picked, 'seq', split_axis=0, concat_axis=0, tiled=True)  10 us
  transfers between devices with their start and end apart: 4, of which 3 were waited for; matrix products, arithmetic and copies ran while one was open for 3% of the time, Pallas kernels for 0%

commit v1 on v0

--- a/solution.py
+++ b/solution.py
@@ -51,7 +51,7 @@
     attended = attended.reshape(row_total, heads_here * head_size)
     out_weight = enc_out.reshape(heads_here * head_size, model_width)
     partial_terms = jnp.dot(attended, out_weight, preferred_element_type=jnp.float32)
-    enc_sum = lax.psum(partial_terms, "head")
+    enc_sum = jnp.sum(lax.all_gather(partial_terms, "head"), axis=0)
     normed = rms_scale(corpus_flat.astype(jnp.float32) + enc_sum, gain_out).astype(jnp.bfloat16)
     memory_cols = heads_here * 2 * head_size
     shard_piece = lax.all_gather(cca_kv, "seq", axis=0, tiled=True)

time: 443 us -> 695 us (1.57)
  waiting for transfers between devices: 298 us -> 522 us
  other arithmetic: 23.7 us -> 51.3 us
    all_gather x0 -> x1, waiting for transfers between devices: none -> 291 us  [on_device(): enc_sum = jnp.sum(lax.all_gather(partial_terms, 'head'), axis=0)]
    psum x1 -> x0, waiting for transfers between devices: 90.3 us -> none  [on_device(): enc_sum = lax.psum(partial_terms, 'head')]
    all_gather x1, waiting for transfers between devices: 0.02 us -> 30.5 us  [on_device(): shard_piece = lax.all_gather(cca_kv, 'seq', axis=0, tiled=True)]
    reduce_sum x0 -> x1, other arithmetic: none -> 24.4 us  [on_device(): enc_sum = jnp.sum(lax.all_gather(partial_terms, 'head'), axis=0)]
    unnamed x21 -> x23, local copies, waits for them, and re-layouts: 18.3 us -> 19.8 us
  transfers between devices with their start and end apart: 4 -> 4, of which waited for: 3 -> 4; matrix products, arithmetic and copies ran while one was open for 3% -> 7% of each run, Pallas kernels for 0% -> 0%
where the time goes in v1:
time: 695 us; the launch traced here: 693 us
  waiting for transfers between devices  522 us (75%)
  local copies, waits for them, and re-layouts  56.1 us (8%)
  other arithmetic  51.3 us (7%)
  matrix products  20.7 us (3%)
  blocking collectives  16.9 us (2%)
  between operations  13.6 us (2%)
  starting transfers between devices  12 us (2%)
    all_gather x1, waiting for transfers between devices, on_device(): enc_sum = jnp.sum(lax.all_gather(partial_terms, 'head'), axis=0)  291 us
    all_to_all x1, waiting for transfers between devices, on_device(): lax.all_to_all(picked, 'seq', split_axis=0, concat_axis=0, tiled=True)  192 us
    all_gather x1, waiting for transfers between devices, on_device(): shard_piece = lax.all_gather(cca_kv, 'seq', axis=0, tiled=True)  30.5 us
    reduce_sum x1, other arithmetic, on_device(): enc_sum = jnp.sum(lax.all_gather(partial_terms, 'head'), axis=0)  24.4 us
    unnamed x23, local copies, waits for them, and re-layouts  19.8 us
    gather x1, local copies, waits for them, and re-layouts, on_device(): jnp.take(memory, lax.all_to_all(wanted, 'seq', split_axis=0, concat_axis=...  18.3 us
    all_to_all x1, blocking collectives, on_device(): lax.all_to_all(wanted, 'seq', split_axis=0, concat_axis=0, tiled=True)  16.9 us
  transfers between devices with their start and end apart: 4, of which 4 were waited for; matrix products, arithmetic and copies ran while one was open for 7% of the time, Pallas kernels for 0%

profile of v1, /device:TPU:104, one launch (start us, length us, event | category | flops | bytes accessed | tf_op | source)
XLA Modules:
  0.0 692.8 jit_solution(4225485770290809380)
XLA Ops:
  6.5 0.7 all-gather.4.cloned.1.call-update
  7.3 16.2 %copy.108 = bf16[4096,2,3,128]{0,3,2,1:T(8,128)(2,1)} copy(bf16[4096,2,3,128]{3,1,2,0:T(2,128)(2,1)} %param.9) | data formatting | bytes 12582912 | tf_op args[1]
  23.5 3.3 fusion.2
  26.9 0.2 copy-done.3
  27.1 1.7 fusion.4
  28.8 1.1 copy-done.4
  29.9 3.5 convolution_convert_fusion
  33.4 1.2 copy.109
  34.5 1.7 reshape.300
  36.3 1.0 fusion.49
  37.2 0.2 copy.129
  37.5 0.2 copy.130
  37.7 0.4 fusion.50
  38.1 0.3 convolution_multiply_fusion.1
  38.4 1.2 fusion.18
  39.6 0.2 copy.114
  39.8 4.4 fusion.21
  44.3 0.7 copy-done.8
  45.1 0.2 convert_reduce_fusion
  45.3 0.1 select_reduce_fusion
  45.4 0.1 all_to_all.13
  45.5 16.9 %all_to_all.20 = s32[32,1,2]{2,1,0:T(1,128)S(1)} all-to-all(s32[32,1,2]{2,1,0:T(1,128)S(1)} %bitcast.92), channel_id=1, replica_groups=mesh['seq'=32,'head'=8] {'seq'}, dimensions={0} | all-to-all | bytes 512 | tf_op jit(solution)/shard_map/all_to_all | solution.py:78
  62.5 0.1 copy.116
  62.6 0.1 reshape.311
  62.7 0.1 copy.107
  62.9 30.5 %all-gather.4.cloned.1.call-done = bf16[4096,2,2,128]{3,2,1,0:T(2,128)(2,1)} async-done(((bf16[128,2,2,128]{3,2,1,0:T(2,128)(2,1)}), bf16[4096,2,2,128]{3,2,1,0:T(2,128)(2,1)}) %all-gather.4.cloned.1.call-update) | async-done | bytes 4194320 | tf_op jit(solution)/shard_map/all_gather | solution.py:57
  93.3 7.2 %reshape.303 = bf16[4096,512]{1,0:T(8,128)(2,1)} reshape(bf16[4096,2,2,128]{3,2,1,0:T(2,128)(2,1)} %all-gather.4.cloned.1.call-done) | data formatting | bytes 8388608 | tf_op jit(solution)/shard_map/reshape | solution.py:60
  100.5 291.3 %all-gather.6.cloned.1.call-done = f32[4096,4096]{1,0:T(8,128)} async-done(((f32[512,4096]{1,0:T(8,128)}), f32[4096,4096]{1,0:T(8,128)}) %all-gather.6.cloned.1.call-update) | async-done | bytes 67108880 | tf_op jit(solution)/shard_map/all_gather | solution.py:54
  391.9 24.4 %reduce_sum.73 = f32[512,4096]{1,0:T(8,128)} reduce(f32[8,512,4096]{2,1,0:T(8,128)} %bitcast.9, f32[]{:T(128)} %constant.68.clone.1), dimensions={0}, to_apply=%region_5.6 | reduce | flops 14680064 | bytes 75497472 | tf_op jit(solution)/shard_map/reduce_sum | solution.py:54
  416.2 5.9 multiply_reduce_fusion
  422.1 1.1 copy-done.2
  423.2 6.0 multiply_convert_fusion
  429.2 5.8 convolution_convert_fusion.1
  435.0 0.1 reshape.304
  435.1 18.3 %gather_fusion = bf16[64,128,2,2,128]{4,3,2,1,0:T(2,128)(2,1)} fusion(bf16[4,128,2,2,128]{4,3,2,1,0:T(2,128)(2,1)S(1)} %reshape.304, s32[1024]{0:T(1024)S(1)} %pad_clamp_fusion.1), kind=kCustom, calls=%fused_computation | custom fusion | bytes 16777472 | tf_op jit(solution)/shard_map/jit(_take)/gather | solution.py:77
  453.5 7.7 %copy_select_fusion = bf16[32,2,128,2,2,128]{5,2,4,3,1,0:T(8,128)(2,1)} fusion(bf16[32,2,128,2,2,128]{5,4,3,2,1,0:T(2,128)(2,1)} %bitcast.83, pred[32,2]{1,0:T(8,128)(4,1)S(1)} %copy.107), kind=kLoop, calls=%fused_computation.10 | loop fusion | flops 4194304 | bytes 16777280 | tf_op jit(solution)/shard_map/jit(_take)/select_n | solution.py:77
  461.2 10.0 %all-to-all-start.1 = ((bf16[32,2,128,2,2,128]{5,2,4,3,1,0:T(8,128)(2,1)}), bf16[32,2,128,2,2,128]{5,2,4,3,1,0:T(8,128)(2,1)}, u32[]{:S(2)}, u32[]{:S(2)}) async-start(bf16[32,2,128,2,2,128]{5,2,4,3,1,0:T(8,128)(2,1)} %copy_select_fusion), calls=%async_computation.1 | async-start | bytes 16777216 | tf_op jit(solution)/shard_map/all_to_all | solution.py:80
  471.8 0.2 maximum_maximum_fusion
  472.0 191.8 %all-to-all-done.1 = bf16[32,2,128,2,2,128]{5,2,4,3,1,0:T(8,128)(2,1)} async-done(((bf16[32,2,128,2,2,128]{5,2,4,3,1,0:T(8,128)(2,1)}), bf16[32,2,128,2,2,128]{5,2,4,3,1,0:T(8,128)(2,1)}, u32[]{:S(2)}, u32[]{:S(2)}) %all-to-all-start.1) | async-done | bytes 8388640 | tf_op jit(solution)/shard_map/all_to_all | solution.py:80
  663.9 4.3 gather_fusion.1
  668.2 0.1 copy.121
  668.4 0.1 slice_select_fusion
  668.5 1.9 collective-permute-start
  670.4 1.6 copy_select_fusion.1
  672.0 7.9 %collective-permute-done = bf16[1,256,2,2,128]{4,1,2,0,3:T(8,128)(2,1)S(1)} collective-permute-done((bf16[1,256,2,2,128]{4,1,2,0,3:T(8,128)(2,1)S(1)}, bf16[1,256,2,2,128]{4,1,2,0,3:T(8,128)(2,1)S(1)}, u32[]{:S(2)}, u32[]{:S(2)}) %collective-permute-start) | collective-permute-done | bytes 262176 | tf_op jit(solution)/shard_map/ppermute | solution.py:15
  679.9 3.1 fusion.55
  682.9 2.0 fusion.15
  685.0 1.0 copy.126
  (42 shorter events, 1.0 us)
Async XLA Ops:
  6.5 33.3 %copy-start = (bf16[2,128,4096]{2,1,0:T(8,128)(2,1)S(1)}, bf16[2,128,4096]{2,1,0:T(8,128)(2,1)}, u32[]{:S(2)}) copy-start(bf16[2,128,4096]{2,1,0:T(8,128)(2,1)} %param.10) | copy-start | bytes 6291460
  6.5 86.8 %all-gather.4.cloned.1.call-start = ((), (), s32[]{:S(2)}) async-start(), calls=%async_computation.2 | async-start | bytes 4325376 | tf_op jit(solution)/shard_map/all_gather | solution.py:57
  7.3 384.6 %all-gather.6.cloned.1.call-start = ((), (), s32[]{:S(2)}) async-start(), calls=%async_computation.3 | async-start | bytes 75497472 | tf_op jit(solution)/shard_map/all_gather | solution.py:54
  7.3 19.6 %copy-start.6 = (f32[4096]{0:T(1024)S(1)}, f32[4096]{0:T(1024)}, u32[]{:S(2)}) copy-start(f32[4096]{0:T(1024)} %param.12) | copy-start | bytes 49156
  23.5 3.5 copy-start.3
  27.1 2.8 copy-start.4
  44.3 0.7 copy-start.8
  416.2 7.0 %copy-start.2 = (f32[512,4096]{1,0:T(8,128)S(1)}, f32[512,4096]{1,0:T(8,128)}, u32[]{:S(2)}) copy-start(f32[512,4096]{1,0:T(8,128)} %reduce_sum.73) | copy-start | bytes 25165828
  416.2 7.0 %copy-start.7 = (f32[4096]{0:T(1024)S(1)}, f32[4096]{0:T(1024)}, u32[]{:S(2)}) copy-start(f32[4096]{0:T(1024)} %param.13) | copy-start | bytes 49156
  461.2 10.3 %copy-start.5 = (bf16[512,2,128]{2,1,0:T(2,128)(2,1)S(1)}, bf16[512,2,128]{2,1,0:T(2,128)(2,1)}, u32[]{:S(2)}) copy-start(bf16[512,2,128]{2,1,0:T(2,128)(2,1)} %param.14) | copy-start | bytes 786436
  461.2 202.6 %all-to-all-start.1 = ((bf16[32,2,128,2,2,128]{5,2,4,3,1,0:T(8,128)(2,1)}), bf16[32,2,128,2,2,128]{5,2,4,3,1,0:T(8,128)(2,1)}, u32[]{:S(2)}, u32[]{:S(2)}) async-start(bf16[32,2,128,2,2,128]{5,2,4,3,1,0:T(8,128)(2,1)} %copy_select_fusion), calls=%async_computation.1 | async-start | bytes 16777216 | tf_op jit(solution)/shard_map/all_to_all | solution.py:80
  668.5 11.4 %collective-permute-start = (bf16[1,256,2,2,128]{4,1,2,0,3:T(8,128)(2,1)S(1)}, bf16[1,256,2,2,128]{4,1,2,0,3:T(8,128)(2,1)S(1)}, u32[]{:S(2)}, u32[]{:S(2)}) collective-permute-start(bf16[1,256,2,2,128]{4,1,2,0,3:T(8,128)(2,1)S(1)} %bitcast.91), channel_id=1, source_target_pairs={{0,8},{8,16},{16,24},{24,32},{32,40},{40,48},{48,56},{56,64},{64,7... | collective-permute-start | bytes 786440 | tf_op jit(solution)/shard_map/ppermute | solution.py:15
  679.9 6.1 copy-start.1
Sparse Core Ops, SparseCore 0:
  9.9 83.3 all-gather.3
  95.2 296.6 all-gather.5
